TPU v7x, 256 devices: a whole 4x4x8 slice. The times are simulated.
256 devices in a mesh: feat: 32 (over y, z), dp: 8 (over x, core).
Axes of the slice: x: 4, y: 4, z: 8, core: 2. Of those that a mesh axis runs over, the one named last changes fastest.
Arguments:
- query_grads: bfloat16 [512, 131072], P(('dp', 'feat')), may hold values from -52 to 52
- build_grads: bfloat16 [1024, 131072], P('dp', 'feat'), may hold values from -52 to 52
- scored_grads: bfloat16 [4096, 131072], P('dp', 'feat'), may hold values from -52 to 52
Outputs:
- scores: float32 [4096, 512], P(('dp', 'feat'))
All inputs are finite; a program needn't handle non-finite values.
Results may differ from a plain program's by a relative error of at most 0.0049.
Values may be sent and summed in bfloat16 or wider, within the bound.
No kernel may reach another device: no remote copies, remote signals or barrier semaphores. Data moves between devices by JAX's collectives and lax.ppermute only.
A program may use at most 128 MiB of HBM per device.

v0:
```python
import functools
import jax
import jax.numpy as jnp
from jax import lax
from jax.sharding import Mesh
from jax.sharding import PartitionSpec as P

FEAT = 131072
FEAT_AXES = ("feat_0", "feat_1")
DP = ("dp_0", "dp_1")
FEAT_DP = ("feat_0", "feat_1", "dp_0", "dp_1")
DP_FEAT = ("dp_0", "dp_1", "feat_0", "feat_1")


def one_axis_at_a_time(shard, axes):
    return functools.reduce(lax.psum, axes, shard)


def sent_to_all(shard, axis):
    size = lax.axis_size(axis)
    return lax.all_to_all(
        jnp.broadcast_to(shard[None], (size, *shard.shape)), axis, 0, 0, tiled=True
    )


def taken_together(shard, axis):
    everything = sent_to_all(shard, axis)
    return jnp.sum(everything, axis=0)


def split_up(shard, dim, size):
    before, after = (shard.shape[:dim], shard.shape[dim + 1 :])
    return jnp.moveaxis(shard.reshape(*before, size, -1, *after), dim, 0)


def sent_and_summed(shard, axis, dim):
    size = lax.axis_size(axis)
    blocks = lax.all_to_all(split_up(shard, dim, size), axis, 0, 0, tiled=True)
    return jnp.sum(blocks, axis=0)


def contract_last(left, right):
    return lax.dot_general(
        left, right, (((1,), (1,)), ((), ())), preferred_element_type=jnp.float32
    )


def on_device(query_grads, build_grads, scored_grads):
    q_local = lax.all_to_all(query_grads, FEAT_AXES, split_axis=1, concat_axis=0, tiled=True)
    gathered = lax.all_gather(build_grads, DP, axis=0, tiled=True)
    build_count = gathered.shape[0]
    cross_part = contract_last(gathered, q_local)
    gram_part = contract_last(gathered, gathered)
    gram_matrix, cross_sums = lax.psum((gram_part, cross_part), FEAT_AXES)
    build_wide = build_grads.astype(jnp.float32)
    square_total = one_axis_at_a_time(jnp.sum(build_wide * build_wide), FEAT_DP)
    damping = 0.1 * square_total / (build_count * FEAT) + 1e-06
    gram_matrix = gram_matrix + build_count * damping * jnp.eye(build_count, dtype=jnp.float32)
    factor = jnp.linalg.cholesky(gram_matrix)
    solved = jax.scipy.linalg.cho_solve((factor, True), cross_sums)
    solved_half = solved.astype(jnp.bfloat16)
    query_wide = q_local.astype(jnp.float32)
    removed = lax.dot_general(
        solved_half, gathered, (((0,), (0,)), ((), ())), preferred_element_type=jnp.float32
    )
    precond = (query_wide - removed) / damping
    self_score = taken_together(jnp.sum(query_wide * precond, axis=1), FEAT_AXES)
    normed = (precond / jnp.sqrt(self_score)[:, None]).astype(jnp.bfloat16)
    partial_value = contract_last(scored_grads, lax.all_gather(normed, DP, axis=0, tiled=True))
    return sent_and_summed(partial_value, FEAT_AXES, 0)


def solution(mesh):
    torus = Mesh(mesh.devices.reshape(4, 8, 4, 2), ("feat_0", "feat_1", "dp_0", "dp_1"))
    in_specs = (P(DP_FEAT, None), P(DP, FEAT_AXES), P(DP, FEAT_AXES))
    out_specs = P(DP_FEAT, None)
    return jax.shard_map(
        on_device, mesh=torus, in_specs=in_specs, out_specs=out_specs, check_vma=False
    )
```

profile of v0, /device:TPU:32, one launch (start us, length us, event | category | flops | bytes accessed | tf_op | source)
XLA Modules:
  0.0 705.6 jit_solution(6234472942404162147)
XLA Ops:
  7.3 29.0 %all_to_all.30 = bf16[2,32,4096]{2,0,1:T(2,128)(2,1)S(1)} all-to-all(bf16[2,32,4096]{2,0,1:T(2,128)(2,1)} %bitcast.141), channel_id=1, replica_groups=mesh['feat_0'=4,'feat_1'=8,'dp_0'=4,'dp_1'=2] {'feat_0','feat_1'}, dimensions={1} | all-to-all | bytes 1048576 | tf_op jit(solution)/shard_map/all_to_all | solution.py:49
  36.5 27.5 %all-gather.3.cloned.1.call-done = bf16[1024,4096]{1,0:T(8,128)(2,1)} async-done(((bf16[128,4096]{1,0:T(8,128)(2,1)}), bf16[1024,4096]{1,0:T(8,128)(2,1)}) %all-gather.3.cloned.1.call-update) | async-done | bytes 8388624 | tf_op jit(solution)/shard_map/all_gather | solution.py:50
  64.0 16.0 %fusion.97 = f32[1024,1024]{0,1:T(8,128)} fusion(bf16[1024,4096]{1,0:T(8,128)(2,1)} %all-gather.3.cloned.1.call-done), kind=kOutput, calls=%fused_computation.222 | convolution fusion | flops 8589934592 | bytes 12582912 | tf_op jit(solution)/shard_map/dot_general | solution.py:43
  85.7 11.1 %psum.43 = f32[]{:T(128)} all-reduce(f32[]{:T(128)} %multiply_reduce_fusion), channel_id=1, replica_groups=mesh['feat_0'=4,'feat_1'=8,'dp_0'=4,'dp_1'=2] {'feat_0'}, use_global_device_ids=true, to_apply=%region_2.0 | all-reduce | flops 1 | bytes 8 | tf_op jit(solution)/shard_map/psum | solution.py:16
  96.8 16.9 %psum.44 = f32[]{:T(128)} all-reduce(f32[]{:T(128)} %psum.43), channel_id=1, replica_groups=mesh['feat_0'=4,'feat_1'=8,'dp_0'=4,'dp_1'=2] {'feat_1'}, use_global_device_ids=true, to_apply=%region_3.0 | all-reduce | flops 1 | bytes 8 | tf_op jit(solution)/shard_map/psum | solution.py:16
  126.7 122.8 %all-reduce.4.cloned.1.call-done = (f32[1024,1024]{0,1:T(8,128)}, f32[1024,64]{0,1:T(8,128)}) async-done(((f32[1024,1024]{0,1:T(8,128)}, f32[1024,64]{0,1:T(8,128)}), (f32[1024,1024]{0,1:T(8,128)}, f32[1024,64]{0,1:T(8,128)})) %all-reduce.4.cloned.1.call-update) | async-done | bytes 4456464 | tf_op jit(solution)/shard_map/psum | solution.py:54
  266.6 11.7 %cholesky.222 = f32[128,128]{1,0:T(8,128)S(1)} custom-call(f32[128,128]{1,0:T(8,128)S(1)} %cholesky.577), custom_call_target="Cholesky" | custom-call | tf_op jit(solution)/shard_map/jit(cholesky)/cholesky | solution.py:59
  278.4 9.8 %custom-call.66 = f32[1,128,128]{1,2,0:T(8,128)S(1)} custom-call(f32[1,128,128]{2,1,0:T(8,128)S(1)} %get-tuple-element.50), custom_call_target="InvertDiagBlocksLowerTriangular" | custom-call | tf_op jit(solution)/shard_map/jit(cholesky)/cholesky | solution.py:59
  291.5 11.7 %cholesky.243 = f32[128,128]{1,0:T(8,128)S(1)} custom-call(f32[128,128]{1,0:T(8,128)S(1)} %cholesky.581), custom_call_target="Cholesky" | custom-call | tf_op jit(solution)/shard_map/jit(cholesky)/cholesky | solution.py:59
  303.5 9.8 %custom-call.67 = f32[1,128,128]{1,2,0:T(8,128)S(1)} custom-call(f32[1,128,128]{2,1,0:T(8,128)S(1)} %get-tuple-element.48), custom_call_target="InvertDiagBlocksLowerTriangular" | custom-call | tf_op jit(solution)/shard_map/jit(cholesky)/cholesky | solution.py:59
  318.9 11.7 %cholesky.466 = f32[128,128]{1,0:T(8,128)S(1)} custom-call(f32[128,128]{1,0:T(8,128)S(1)} %cholesky.586), custom_call_target="Cholesky" | custom-call | tf_op jit(solution)/shard_map/jit(cholesky)/cholesky | solution.py:59
  331.3 9.8 %custom-call.68 = f32[1,128,128]{1,2,0:T(8,128)S(1)} custom-call(f32[1,128,128]{2,1,0:T(8,128)S(1)} %get-tuple-element.46), custom_call_target="InvertDiagBlocksLowerTriangular" | custom-call | tf_op jit(solution)/shard_map/jit(cholesky)/cholesky | solution.py:59
  345.7 11.7 %cholesky.485 = f32[128,128]{1,0:T(8,128)S(1)} custom-call(f32[128,128]{1,0:T(8,128)S(1)} %cholesky.591), custom_call_target="Cholesky" | custom-call | tf_op jit(solution)/shard_map/jit(cholesky)/cholesky | solution.py:59
  372.3 12.1 %cholesky.504 = f32[128,128]{1,0:T(8,128)S(1)} custom-call(f32[128,128]{1,0:T(8,128)S(1)} %cholesky.596), custom_call_target="Cholesky" | custom-call | tf_op jit(solution)/shard_map/jit(cholesky)/cholesky | solution.py:59
  385.2 9.8 %custom-call.70 = f32[1,128,128]{1,2,0:T(8,128)S(1)} custom-call(f32[1,128,128]{2,1,0:T(8,128)S(1)} %get-tuple-element.42), custom_call_target="InvertDiagBlocksLowerTriangular" | custom-call | tf_op jit(solution)/shard_map/jit(cholesky)/cholesky | solution.py:59
  399.3 11.7 %cholesky.524 = f32[128,128]{1,0:T(8,128)S(1)} custom-call(f32[128,128]{1,0:T(8,128)S(1)} %cholesky.601), custom_call_target="Cholesky" | custom-call | tf_op jit(solution)/shard_map/jit(cholesky)/cholesky | solution.py:59
  411.8 9.8 %custom-call.71 = f32[1,128,128]{1,2,0:T(8,128)S(1)} custom-call(f32[1,128,128]{2,1,0:T(8,128)S(1)} %get-tuple-element.40), custom_call_target="InvertDiagBlocksLowerTriangular" | custom-call | tf_op jit(solution)/shard_map/jit(cholesky)/cholesky | solution.py:59
  425.4 11.7 %cholesky.544 = f32[128,128]{1,0:T(8,128)S(1)} custom-call(f32[128,128]{1,0:T(8,128)S(1)} %cholesky.606), custom_call_target="Cholesky" | custom-call | tf_op jit(solution)/shard_map/jit(cholesky)/cholesky | solution.py:59
  450.7 11.7 %cholesky.562 = f32[128,128]{1,0:T(8,128)S(1)} custom-call(f32[128,128]{1,0:T(8,128)S(1)} %convolution_subtract_fusion.7), custom_call_target="Cholesky" | custom-call | tf_op jit(solution)/shard_map/jit(cholesky)/cholesky | solution.py:59
  477.6 24.0 %while.1 = (s32[]{:T(128)}, f32[1024,1024]{0,1:T(8,128)}, s32[8,2]{0,1:T(2,128)S(1)}, f32[8,128,128]{2,1,0:T(8,128)S(1)}, s32[]{:T(128)}) while((s32[]{:T(128)}, f32[1024,1024]{0,1:T(8,128)}, s32[8,2]{0,1:T(2,128)S(1)}, f32[8,128,128]{2,1,0:T(8,128)S(1)}, s32[]{:T(128)}) %tuple.53), condition=%wide.while_cond, body=%wide.while_body.sunk | while | flops 2 | bytes 393329 | solution.py:60
  501.5 78.8 %custom-call.73 = f32[8,128,128]{1,2,0:T(8,128)S(1)} custom-call(f32[8,128,128]{2,1,0:T(8,128)S(1)} %get-tuple-element.12), custom_call_target="InvertDiagBlocksLowerTriangular" | custom-call | tf_op jit(solution)/shard_map/jit(_cho_solve)/triangular_solve | solution.py:60
  607.7 14.9 %all_to_all.31 = f32[32,1,64]{2,1,0:T(1,128)S(1)} all-to-all(f32[32,1,64]{2,1,0:T(1,128)S(1)} %broadcast_in_dim.4), channel_id=1, replica_groups=mesh['feat_0'=4,'feat_1'=8,'dp_0'=4,'dp_1'=2] {'feat_0','feat_1'}, dimensions={0} | all-to-all | bytes 16384 | tf_op jit(solution)/shard_map/all_to_all | solution.py:21
  623.6 30.1 %all-gather.5.cloned.1.call-done = bf16[512,4096]{1,0:T(8,128)(2,1)} async-done(((bf16[64,4096]{1,0:T(8,128)(2,1)}), bf16[512,4096]{1,0:T(8,128)(2,1)}) %all-gather.5.cloned.1.call-update) | async-done | bytes 4194320 | tf_op jit(solution)/shard_map/all_gather | solution.py:69
  659.6 38.6 %all_to_all.32 = f32[32,16,512]{2,1,0:T(8,128)S(1)} all-to-all(f32[32,16,512]{2,1,0:T(8,128)S(1)} %bitcast.140), channel_id=1, replica_groups=mesh['feat_0'=4,'feat_1'=8,'dp_0'=4,'dp_1'=2] {'feat_0','feat_1'}, dimensions={0} | all-to-all | bytes 2097152 | tf_op jit(solution)/shard_map/all_to_all | solution.py:38
  (183 shorter events, 157.1 us)
Async XLA Ops:
  6.5 57.5 %all-gather.3.cloned.1.call-start = ((), (), s32[]{:S(2)}) async-start(), calls=%async_computation.3 | async-start | bytes 9437184 | tf_op jit(solution)/shard_map/all_gather | solution.py:50
  7.3 242.2 %all-reduce.4.cloned.1.call-start = ((), (), s32[]{:S(2)}) async-start(), calls=%async_computation.5 | async-start | bytes 8912896 | tf_op jit(solution)/shard_map/psum | solution.py:54
  64.0 16.0 %copy-start = (bf16[1024,4096]{1,0:T(8,128)(2,1)S(1)}, bf16[1024,4096]{1,0:T(8,128)(2,1)}, u32[]{:S(2)}) copy-start(bf16[1024,4096]{1,0:T(8,128)(2,1)} %all-gather.3.cloned.1.call-done) | copy-start | bytes 25165828
  83.3 1.2 copy-start.3
  83.4 570.4 %all-gather.5.cloned.1.call-start = ((), (), s32[]{:S(2)}) async-start(), calls=%async_computation.4 | async-start | bytes 4718592 | tf_op jit(solution)/shard_map/all_gather | solution.py:69
  264.6 2.0 copy-start.2
  314.5 2.0 copy-start.1
  472.6 107.7 %copy-start.4 = (f32[1024,64]{0,1:T(8,128)S(1)}, f32[1024,64]{0,1:T(8,128)}, u32[]{:S(2)}) copy-start(f32[1024,64]{0,1:T(8,128)} %get-tuple-element.34) | copy-start | bytes 786436
Sparse Core Ops, SparseCore 0:
  9.2 54.7 all-gather.2
  83.5 165.9 all-reduce.3
  623.7 29.9 all-gather.4
where the time goes:
time: 713 us; the launch traced here: 706 us
  other arithmetic  263 us (37%)
  waiting for transfers between devices  181 us (25%)
  blocking collectives  123 us (17%)
  matrix products  77.9 us (11%)
  local copies, waits for them, and re-layouts  40.5 us (6%)
  between operations  19.6 us (3%)
    another operation x30, other arithmetic, on_device(): factor = jnp.linalg.cholesky(gram_matrix)  168 us
    psum x1, waiting for transfers between devices, on_device(): gram_matrix, cross_sums = lax.psum((gram_part, cross_part), FEAT_AXES)  123 us
    another operation x4, other arithmetic, on_device(): solved = jax.scipy.linalg.cho_solve((factor, True), cross_sums)  83.7 us
    psum x4, blocking collectives, one_axis_at_a_time(): return functools.reduce(lax.psum, axes, shard)  40.4 us
    all_to_all x1, blocking collectives, sent_and_summed(): blocks = lax.all_to_all(split_up(shard, dim, size), axis, 0, 0, tiled=True)  38.6 us
    all_gather x1, waiting for transfers between devices, on_device(): lax.all_gather(normed, DP, axis=0, tiled=True)  30.1 us
    all_to_all x1, blocking collectives, on_device(): lax.all_to_all(query_grads, FEAT_AXES, split_axis=1, concat_axis=0, tiled...  29 us
    all_gather x1, waiting for transfers between devices, on_device(): gathered = lax.all_gather(build_grads, DP, axis=0, tiled=True)  27.5 us
  transfers between devices with their start and end apart: 3, of which 3 were waited for; matrix products, arithmetic and copies ran while one was open for 0% of the time, Pallas kernels for 0%

commit v1 on v0

--- a/solution.py
+++ b/solution.py
@@ -51,7 +51,7 @@
     build_count = gathered.shape[0]
     cross_part = contract_last(gathered, q_local)
     gram_part = contract_last(gathered, gathered)
-    gram_matrix, cross_sums = lax.psum((gram_part, cross_part), FEAT_AXES)
+    gram_matrix, cross_sums = lax.psum(lax.psum((gram_part, cross_part), "feat_0"), "feat_1")
     build_wide = build_grads.astype(jnp.float32)
     square_total = one_axis_at_a_time(jnp.sum(build_wide * build_wide), FEAT_DP)
     damping = 0.1 * square_total / (build_count * FEAT) + 1e-06

time: 713 us -> 767 us (1.076)
  waiting for transfers between devices: 181 us -> 233 us
    psum x1 -> x2, waiting for transfers between devices: 123 us -> 175 us  [the longest x1 103 us: on_device(): lax.psum((gram_part, cross_part), 'feat_0')]
  transfers between devices with their start and end apart: 3 -> 4, of which waited for: 3 -> 4; matrix products, arithmetic and copies ran while one was open for 0% -> 0% of each run, Pallas kernels for 0% -> 0%
where the time goes in v1:
time: 767 us; the launch traced here: 759 us
  other arithmetic  263 us (34%)
  waiting for transfers between devices  233 us (30%)
  blocking collectives  126 us (16%)
  matrix products  77.9 us (10%)
  local copies, waits for them, and re-layouts  39.3 us (5%)
  between operations  19.6 us (3%)
    another operation x30, other arithmetic, on_device(): factor = jnp.linalg.cholesky(gram_matrix)  168 us
    psum x1, waiting for transfers between devices, on_device(): lax.psum((gram_part, cross_part), 'feat_0')  103 us
    another operation x4, other arithmetic, on_device(): solved = jax.scipy.linalg.cho_solve((factor, True), cross_sums)  83.7 us
    psum x1, waiting for transfers between devices, on_device(): lax.psum(lax.psum((gram_part, cross_part), 'feat_0'), 'feat_1')  72.3 us
    psum x4, blocking collectives, one_axis_at_a_time(): return functools.reduce(lax.psum, axes, shard)  40.5 us
    all_to_all x1, blocking collectives, sent_and_summed(): blocks = lax.all_to_all(split_up(shard, dim, size), axis, 0, 0, tiled=True)  38.6 us
    all_gather x1, waiting for transfers between devices, on_device(): lax.all_gather(normed, DP, axis=0, tiled=True)  30.1 us
    all_to_all x1, blocking collectives, on_device(): lax.all_to_all(query_grads, FEAT_AXES, split_axis=1, concat_axis=0, tiled...  29 us
  transfers between devices with their start and end apart: 4, of which 4 were waited for; matrix products, arithmetic and copies ran while one was open for 0% of the time, Pallas kernels for 0%

profile of v1, /device:TPU:32, one launch (start us, length us, event | category | flops | bytes accessed | tf_op | source)
XLA Modules:
  0.0 759.4 jit_solution(10800764814481311799)
XLA Ops:
  7.3 29.0 %all_to_all.30 = bf16[2,32,4096]{2,0,1:T(2,128)(2,1)S(1)} all-to-all(bf16[2,32,4096]{2,0,1:T(2,128)(2,1)} %bitcast.141), channel_id=1, replica_groups=mesh['feat_0'=4,'feat_1'=8,'dp_0'=4,'dp_1'=2] {'feat_0','feat_1'}, dimensions={1} | all-to-all | bytes 1048576 | tf_op jit(solution)/shard_map/all_to_all | solution.py:49
  36.5 27.5 %all-gather.3.cloned.1.call-done = bf16[1024,4096]{1,0:T(8,128)(2,1)} async-done(((bf16[128,4096]{1,0:T(8,128)(2,1)}), bf16[1024,4096]{1,0:T(8,128)(2,1)}) %all-gather.3.cloned.1.call-update) | async-done | bytes 8388624 | tf_op jit(solution)/shard_map/all_gather | solution.py:50
  64.0 15.9 %fusion.97 = f32[1024,1024]{0,1:T(8,128)} fusion(bf16[1024,4096]{1,0:T(8,128)(2,1)} %all-gather.3.cloned.1.call-done), kind=kOutput, calls=%fused_computation.222 | convolution fusion | flops 8589934592 | bytes 12582912 | tf_op jit(solution)/shard_map/dot_general | solution.py:43
  83.4 102.5 %all-reduce.8.cloned.1.call-done = (f32[1024,1024]{0,1:T(8,128)}, f32[1024,64]{0,1:T(8,128)}) async-done(((f32[1024,1024]{0,1:T(8,128)}, f32[1024,64]{0,1:T(8,128)}), (f32[1024,1024]{0,1:T(8,128)}, f32[1024,64]{0,1:T(8,128)})) %all-reduce.8.cloned.1.call-update) | async-done | bytes 4456464 | tf_op jit(solution)/shard_map/psum | solution.py:54
  196.3 17.0 %psum.59 = f32[]{:T(128)} all-reduce(f32[]{:T(128)} %psum.58), channel_id=1, replica_groups=mesh['feat_0'=4,'feat_1'=8,'dp_0'=4,'dp_1'=2] {'feat_1'}, use_global_device_ids=true, to_apply=%region_4.0 | all-reduce | flops 1 | bytes 8 | tf_op jit(solution)/shard_map/psum | solution.py:16
  213.3 11.2 %psum.60 = f32[]{:T(128)} all-reduce(f32[]{:T(128)} %psum.59), channel_id=1, replica_groups=mesh['feat_0'=4,'feat_1'=8,'dp_0'=4,'dp_1'=2] {'dp_0'}, use_global_device_ids=true, to_apply=%region_5.0 | all-reduce | flops 1 | bytes 8 | tf_op jit(solution)/shard_map/psum | solution.py:16
  228.3 72.3 %all-reduce.6.cloned.1.call-done = (f32[1024,1024]{0,1:T(8,128)}, f32[1024,64]{0,1:T(8,128)}) async-done(((f32[1024,1024]{0,1:T(8,128)}, f32[1024,64]{0,1:T(8,128)}), (f32[1024,1024]{0,1:T(8,128)}, f32[1024,64]{0,1:T(8,128)})) %all-reduce.6.cloned.1.call-update) | async-done | bytes 4456464 | tf_op jit(solution)/shard_map/psum | solution.py:54
  317.6 11.7 %cholesky.222 = f32[128,128]{1,0:T(8,128)S(1)} custom-call(f32[128,128]{1,0:T(8,128)S(1)} %cholesky.577), custom_call_target="Cholesky" | custom-call | tf_op jit(solution)/shard_map/jit(cholesky)/cholesky | solution.py:59
  329.5 9.8 %custom-call.66 = f32[1,128,128]{1,2,0:T(8,128)S(1)} custom-call(f32[1,128,128]{2,1,0:T(8,128)S(1)} %get-tuple-element.52), custom_call_target="InvertDiagBlocksLowerTriangular" | custom-call | tf_op jit(solution)/shard_map/jit(cholesky)/cholesky | solution.py:59
  342.6 11.7 %cholesky.243 = f32[128,128]{1,0:T(8,128)S(1)} custom-call(f32[128,128]{1,0:T(8,128)S(1)} %cholesky.581), custom_call_target="Cholesky" | custom-call | tf_op jit(solution)/shard_map/jit(cholesky)/cholesky | solution.py:59
  354.6 9.8 %custom-call.67 = f32[1,128,128]{1,2,0:T(8,128)S(1)} custom-call(f32[1,128,128]{2,1,0:T(8,128)S(1)} %get-tuple-element.50), custom_call_target="InvertDiagBlocksLowerTriangular" | custom-call | tf_op jit(solution)/shard_map/jit(cholesky)/cholesky | solution.py:59
  369.9 11.7 %cholesky.466 = f32[128,128]{1,0:T(8,128)S(1)} custom-call(f32[128,128]{1,0:T(8,128)S(1)} %cholesky.586), custom_call_target="Cholesky" | custom-call | tf_op jit(solution)/shard_map/jit(cholesky)/cholesky | solution.py:59
  396.8 11.7 %cholesky.485 = f32[128,128]{1,0:T(8,128)S(1)} custom-call(f32[128,128]{1,0:T(8,128)S(1)} %cholesky.591), custom_call_target="Cholesky" | custom-call | tf_op jit(solution)/shard_map/jit(cholesky)/cholesky | solution.py:59
  409.3 9.8 %custom-call.69 = f32[1,128,128]{1,2,0:T(8,128)S(1)} custom-call(f32[1,128,128]{2,1,0:T(8,128)S(1)} %get-tuple-element.46), custom_call_target="InvertDiagBlocksLowerTriangular" | custom-call | tf_op jit(solution)/shard_map/jit(cholesky)/cholesky | solution.py:59
  423.4 12.1 %cholesky.504 = f32[128,128]{1,0:T(8,128)S(1)} custom-call(f32[128,128]{1,0:T(8,128)S(1)} %cholesky.596), custom_call_target="Cholesky" | custom-call | tf_op jit(solution)/shard_map/jit(cholesky)/cholesky | solution.py:59
  436.3 9.8 %custom-call.70 = f32[1,128,128]{1,2,0:T(8,128)S(1)} custom-call(f32[1,128,128]{2,1,0:T(8,128)S(1)} %get-tuple-element.44), custom_call_target="InvertDiagBlocksLowerTriangular" | custom-call | tf_op jit(solution)/shard_map/jit(cholesky)/cholesky | solution.py:59
  450.4 11.7 %cholesky.524 = f32[128,128]{1,0:T(8,128)S(1)} custom-call(f32[128,128]{1,0:T(8,128)S(1)} %cholesky.601), custom_call_target="Cholesky" | custom-call | tf_op jit(solution)/shard_map/jit(cholesky)/cholesky | solution.py:59
  476.5 11.7 %cholesky.544 = f32[128,128]{1,0:T(8,128)S(1)} custom-call(f32[128,128]{1,0:T(8,128)S(1)} %cholesky.606), custom_call_target="Cholesky" | custom-call | tf_op jit(solution)/shard_map/jit(cholesky)/cholesky | solution.py:59
  501.8 11.7 %cholesky.562 = f32[128,128]{1,0:T(8,128)S(1)} custom-call(f32[128,128]{1,0:T(8,128)S(1)} %convolution_subtract_fusion.7), custom_call_target="Cholesky" | custom-call | tf_op jit(solution)/shard_map/jit(cholesky)/cholesky | solution.py:59
  528.6 24.0 %while.1 = (s32[]{:T(128)}, f32[1024,1024]{0,1:T(8,128)}, s32[8,2]{0,1:T(2,128)S(1)}, f32[8,128,128]{2,1,0:T(8,128)S(1)}, s32[]{:T(128)}) while((s32[]{:T(128)}, f32[1024,1024]{0,1:T(8,128)}, s32[8,2]{0,1:T(2,128)S(1)}, f32[8,128,128]{2,1,0:T(8,128)S(1)}, s32[]{:T(128)}) %tuple.53), condition=%wide.while_cond, body=%wide.while_body.sunk | while | flops 2 | bytes 393329 | solution.py:60
  552.6 78.8 %custom-call.73 = f32[8,128,128]{1,2,0:T(8,128)S(1)} custom-call(f32[8,128,128]{2,1,0:T(8,128)S(1)} %get-tuple-element.12), custom_call_target="InvertDiagBlocksLowerTriangular" | custom-call | tf_op jit(solution)/shard_map/jit(_cho_solve)/triangular_solve | solution.py:60
  658.8 17.6 %all_to_all.31 = f32[32,1,64]{2,1,0:T(1,128)S(1)} all-to-all(f32[32,1,64]{2,1,0:T(1,128)S(1)} %broadcast_in_dim.4), channel_id=1, replica_groups=mesh['feat_0'=4,'feat_1'=8,'dp_0'=4,'dp_1'=2] {'feat_0','feat_1'}, dimensions={0} | all-to-all | bytes 16384 | tf_op jit(solution)/shard_map/all_to_all | solution.py:21
  677.4 30.1 %all-gather.5.cloned.1.call-done = bf16[512,4096]{1,0:T(8,128)(2,1)} async-done(((bf16[64,4096]{1,0:T(8,128)(2,1)}), bf16[512,4096]{1,0:T(8,128)(2,1)}) %all-gather.5.cloned.1.call-update) | async-done | bytes 4194320 | tf_op jit(solution)/shard_map/all_gather | solution.py:69
  713.4 38.6 %all_to_all.32 = f32[32,16,512]{2,1,0:T(8,128)S(1)} all-to-all(f32[32,16,512]{2,1,0:T(8,128)S(1)} %bitcast.140), channel_id=1, replica_groups=mesh['feat_0'=4,'feat_1'=8,'dp_0'=4,'dp_1'=2] {'feat_0','feat_1'}, dimensions={0} | all-to-all | bytes 2097152 | tf_op jit(solution)/shard_map/all_to_all | solution.py:38
  (186 shorter events, 165.6 us)
Async XLA Ops:
  6.5 57.5 %all-gather.3.cloned.1.call-start = ((), (), s32[]{:S(2)}) async-start(), calls=%async_computation.3 | async-start | bytes 9437184 | tf_op jit(solution)/shard_map/all_gather | solution.py:50
  7.3 178.6 %all-reduce.8.cloned.1.call-start = ((), (), s32[]{:S(2)}) async-start(), calls=%async_computation.6 | async-start | bytes 8912896 | tf_op jit(solution)/shard_map/psum | solution.py:54
  64.0 15.9 %copy-start = (bf16[1024,4096]{1,0:T(8,128)(2,1)S(1)}, bf16[1024,4096]{1,0:T(8,128)(2,1)}, u32[]{:S(2)}) copy-start(bf16[1024,4096]{1,0:T(8,128)(2,1)} %all-gather.3.cloned.1.call-done) | copy-start | bytes 25165828
  83.3 102.7 %copy-start.3 = (bf16[128,4096]{1,0:T(8,128)(2,1)S(1)}, bf16[128,4096]{1,0:T(8,128)(2,1)}, u32[]{:S(2)}) copy-start(bf16[128,4096]{1,0:T(8,128)(2,1)} %param.4) | copy-start | bytes 3145732
  83.3 217.2 %all-reduce.6.cloned.1.call-start = ((), (), s32[]{:S(2)}) async-start(), calls=%async_computation.5 | async-start | bytes 8912896 | tf_op jit(solution)/shard_map/psum | solution.py:54
  185.9 521.6 %all-gather.5.cloned.1.call-start = ((), (), s32[]{:S(2)}) async-start(), calls=%async_computation.4 | async-start | bytes 4718592 | tf_op jit(solution)/shard_map/all_gather | solution.py:69
  315.6 2.0 copy-start.2
  365.5 2.0 copy-start.1
  523.7 107.7 %copy-start.4 = (f32[1024,64]{0,1:T(8,128)S(1)}, f32[1024,64]{0,1:T(8,128)}, u32[]{:S(2)}) copy-start(f32[1024,64]{0,1:T(8,128)} %get-tuple-element.34) | copy-start | bytes 786436
Sparse Core Ops, SparseCore 0:
  9.2 54.7 all-gather.2
  83.4 102.3 all-reduce.7
  188.3 112.1 all-reduce.5
  677.6 29.9 all-gather.4
